TPU v7x, 32 devices: a whole 2x2x4 slice. The times are simulated.
32 devices in a mesh: groups: 2 (over y), slide: 4 (over z), rep: 2 (over x), chan: 2 (over core).
Axes of the slice: x: 2, y: 2, z: 4, core: 2. Of those that a mesh axis runs over, the one named last changes fastest.
Arguments:
- tile_pixels: bfloat16 [4, 64, 6144], P(('groups', 'rep'), ('slide', 'chan')), parts along dimension 0, may hold values from -6 to 6
- tile_cell: int32 [4, 64], P(('groups', 'rep'), ('slide', 'chan')), parts along dimension 0, may hold values from -1 to 2047, as said below
- agg_cot: float32 [4, 64, 192, 128], P(('groups', 'rep'), 'slide', 'chan'), parts along dimension 0, may hold values from -6 to 6
- dw_weight: float32 [49, 96], replicated, may hold values from -0.6 to 0.6
- norm_gain: float32 [96], replicated, may hold values from 0.25 to 1.75
- up_weight: bfloat16 [96, 384], replicated, may hold values from -0.625 to 0.625
- proj_weight: bfloat16 [384, 96], replicated, may hold values from -0.3125 to 0.3125
- layer_scale: float32 [96], replicated, may hold values from 0.3 to 1
- ds_gain: float32 [96], replicated, may hold values from 0.25 to 1.75
- ds_weight: bfloat16 [384, 192], replicated, may hold values from -0.3125 to 0.3125
- agg_weight: bfloat16 [9, 192, 192], P(None, None, 'chan'), may hold values from -0.15625 to 0.15625
Outputs:
- agg_map: bfloat16 [4, 64, 192, 128], P(('groups', 'rep'), 'slide', 'chan'), parts along dimension 0
- agg_grad: float32 [18, 192, 192], P('groups', None, 'chan'), parts along dimension 0
- dw_grad: float32 [98, 96], P('groups'), parts along dimension 0
- up_grad: float32 [192, 384], P('groups'), parts along dimension 0
- proj_grad: float32 [768, 96], P('groups'), parts along dimension 0
- ds_grad: float32 [768, 192], P('groups'), parts along dimension 0
There are 2 independent parts, one for each index of `groups`. A program takes and returns all parts, laid end to end along the dimension named above; an argument that names none is the same for every part. Nothing has to cross between parts.
Inputs may be any that keep to these rules, and one draw needn't show every extreme that they name: `tile_cell`: A value r * 64 + q names a tile of grid row r and column q of a 32 x 64 slide grid; -1 marks an empty slot. No cell appears twice in one slide. Of the slots of one device (8 consecutive slots), at most 2 lie in one band of 8 tile rows, and in every slide one band holds exactly 2 tiles from every device.
All inputs are finite; a program needn't handle non-finite values.
Results may differ from a plain program's by a relative error of at most 0.018.
Values may be sent and summed in bfloat16 or wider, within the bound.
No kernel may reach another device: no remote copies, remote signals or barrier semaphores. Data moves between devices by JAX's collectives and lax.ppermute only.
A program may use at most 128 MiB of HBM per device.

v0:
```python
import math
import jax
import jax.numpy as jnp
from jax import lax
from jax.sharding import PartitionSpec as P

TILE_SIDE = 8
CAP = 2
GR = 8
GW = 64
BAND_CELLS = 512
FEAT = 3072


def shifted(value, axis, steps):
    count = lax.axis_size(axis)
    first, last = (max(0, -steps), min(count, count - steps))
    return lax.ppermute(value, axis, [(source, source + steps) for source in range(first, last)])


def layer_norm(values, gain):
    center = values - jnp.mean(values, axis=-1, keepdims=True)
    spread = jnp.mean(center * center, axis=-1, keepdims=True)
    return center * lax.rsqrt(spread + 1e-06) * gain


def stem(params, tile_rows):
    dw_weight, norm_gain, up_weight, proj_weight, layer_scale, ds_gain, ds_weight = params
    tile_count = tile_rows.shape[0]
    tile_side = TILE_SIDE
    channels = dw_weight.shape[1]
    inputs = tile_rows.reshape(tile_count, tile_side, tile_side, channels).astype(jnp.float32)
    padded = jnp.pad(inputs, ((0, 0), (3, 3), (3, 3), (0, 0)))
    spatial = jnp.zeros_like(inputs)
    for row_tap in range(7):
        for col_tap in range(7):
            spatial = (
                spatial
                + dw_weight[row_tap * 7 + col_tap]
                * padded[:, row_tap : row_tap + tile_side, col_tap : col_tap + tile_side, :]
            )
    normed = (
        layer_norm(spatial, norm_gain)
        .reshape(tile_count * tile_side * tile_side, channels)
        .astype(jnp.bfloat16)
    )
    hidden = jax.nn.gelu(
        jnp.dot(normed, up_weight, preferred_element_type=jnp.float32), approximate=False
    ).astype(jnp.bfloat16)
    branch = jnp.dot(hidden, proj_weight, preferred_element_type=jnp.float32)
    mixed_rows = inputs.reshape(tile_count * tile_side * tile_side, channels) + layer_scale * branch
    lowered = layer_norm(mixed_rows, ds_gain).astype(jnp.bfloat16)
    half_side = tile_side // 2
    patches = lowered.reshape(tile_count, half_side, 2, half_side, 2, channels).transpose(
        0, 1, 3, 2, 4, 5
    )
    patches = patches.reshape(tile_count * half_side * half_side, 4 * channels)
    result = jnp.dot(patches, ds_weight, preferred_element_type=jnp.float32)
    return result.reshape(tile_count, half_side * half_side * ds_weight.shape[1])


def aggregate(padded, weight_half):
    out_rows = (padded.shape[0] - 1) // 2
    out_cols = (padded.shape[1] - 1) // 2
    accumulated = jnp.zeros((out_rows * out_cols, weight_half.shape[2]), jnp.float32)
    for row_tap in range(3):
        for col_tap in range(3):
            window = padded[
                row_tap : row_tap + 2 * out_rows - 1 : 2,
                col_tap : col_tap + 2 * out_cols - 1 : 2,
                :,
            ]
            accumulated = accumulated + jnp.dot(
                window.reshape(out_rows * out_cols, padded.shape[2]),
                weight_half[row_tap * 3 + col_tap],
                preferred_element_type=jnp.float32,
            )
    return accumulated.reshape(out_rows, out_cols, weight_half.shape[2])


def on_device(
    tile_pixels,
    tile_cell,
    agg_cot,
    dw_weight,
    norm_gain,
    up_weight,
    proj_weight,
    layer_scale,
    ds_gain,
    ds_weight,
    agg_weight,
):
    params = (dw_weight, norm_gain, up_weight, proj_weight, layer_scale, ds_gain, ds_weight)
    tile_rows = tile_pixels[0]
    cell_ids = tile_cell[0]
    band_count = lax.axis_size("slide")
    chan_count = lax.axis_size("chan")
    feat_side = TILE_SIDE // 2
    checked_stem = jax.checkpoint(stem)
    tile_out, pull_stem = jax.vjp(lambda chosen: checked_stem(chosen, tile_rows), params)
    features = tile_out.astype(jnp.bfloat16)
    present = cell_ids >= 0
    dest_band = jnp.where(present, cell_ids // BAND_CELLS, band_count)
    within = jnp.where(present, cell_ids % BAND_CELLS, BAND_CELLS)
    slot_order = jnp.arange(cell_ids.shape[0], dtype=jnp.int32)
    earlier = (dest_band[:, None] == dest_band[None, :]) & (
        slot_order[None, :] < slot_order[:, None]
    )
    place_rank = jnp.sum(earlier.astype(jnp.int32), axis=1)
    position = jnp.where(present, dest_band * CAP + place_rank, band_count * CAP)
    send_rows = (
        jnp.zeros((band_count * CAP, FEAT), jnp.bfloat16).at[position].set(features, mode="drop")
    )
    send_cells = (
        jnp.full((band_count * CAP,), BAND_CELLS, jnp.int32).at[position].set(within, mode="drop")
    )
    own_rows, own_cells = (
        lax.all_to_all(send_rows, "slide", split_axis=0, concat_axis=0, tiled=True),
        lax.all_to_all(send_cells, "slide", split_axis=0, concat_axis=0, tiled=True),
    )
    recv_rows, recv_cells = (
        lax.all_gather(own_rows, "chan", axis=0, tiled=True),
        lax.all_gather(own_cells, "chan", axis=0, tiled=True),
    )
    cells_map = (
        jnp.zeros((BAND_CELLS, FEAT), jnp.bfloat16).at[recv_cells].set(recv_rows, mode="drop")
    )
    band_grid = cells_map.reshape(GR, GW, feat_side, feat_side, -1).transpose(0, 2, 1, 3, 4)
    band_grid = band_grid.reshape(GR * feat_side, GW * feat_side, -1)
    top_row = shifted(band_grid[-1], "slide", 1)
    padded = jnp.pad(jnp.concatenate([top_row[None], band_grid], axis=0), ((0, 0), (1, 0), (0, 0)))
    total_rows = agg_cot.shape[1] * band_count * lax.axis_size("rep") * agg_cot.shape[3]
    loss_scale = 1.0 / math.sqrt(total_rows)
    cotangent = agg_cot[0].transpose(0, 2, 1) * loss_scale
    result, pull_agg = jax.vjp(aggregate, padded, agg_weight)
    agg_map = result.astype(jnp.bfloat16).transpose(0, 2, 1)[None]
    d_padded, d_weight = pull_agg(cotangent)
    from_below = shifted(d_padded[0, 1:], "slide", -1)
    map_grad = (
        d_padded[1:, 1:]
        .astype(jnp.float32)
        .at[-1]
        .add(from_below.astype(jnp.float32))
        .astype(jnp.bfloat16)
    )
    grad_cells = (
        map_grad.reshape(GR, feat_side, GW, feat_side, -1)
        .transpose(0, 2, 1, 3, 4)
        .reshape(BAND_CELLS, FEAT)
    )
    slot_grads = jnp.where(
        (recv_cells < BAND_CELLS)[:, None],
        grad_cells[jnp.minimum(recv_cells, BAND_CELLS - 1)],
        jnp.zeros((), jnp.bfloat16),
    )
    by_source = slot_grads.reshape(chan_count, band_count, CAP, FEAT).transpose(1, 0, 2, 3)
    by_source = by_source.reshape(band_count * chan_count * CAP, FEAT)
    arrived = lax.all_to_all(by_source, "slide", split_axis=0, concat_axis=0, tiled=True)
    arrived = arrived.reshape(band_count, chan_count, CAP, FEAT).astype(jnp.float32)
    summed = lax.psum_scatter(
        arrived.astype(jnp.bfloat16), "chan", scatter_dimension=1, tiled=True
    ).astype(jnp.float32)
    gathered_grads = summed.reshape(band_count * CAP, FEAT)
    feature_grad = jnp.where(
        present[:, None], gathered_grads[jnp.minimum(position, band_count * CAP - 1)], 0.0
    )
    stem_grads = pull_stem(feature_grad)[0]
    dw_term = stem_grads[0]
    up_term = stem_grads[2].astype(jnp.float32)
    proj_term = stem_grads[3].astype(jnp.float32)
    ds_term = stem_grads[6].astype(jnp.float32)
    agg_term = d_weight.astype(jnp.float32)
    half_width = agg_term.shape[2]
    embedded = lax.dynamic_update_slice(
        jnp.zeros((9, agg_term.shape[1], half_width * chan_count), jnp.float32),
        agg_term,
        (0, 0, lax.axis_index("chan") * half_width),
    )
    summed_all = lax.psum(
        (dw_term, up_term, proj_term, ds_term, embedded), ("slide", "rep", "chan")
    )
    dw_grad = summed_all[0]
    up_grad = summed_all[1]
    proj_grad = summed_all[2]
    ds_grad = summed_all[3]
    agg_grad = lax.dynamic_slice_in_dim(
        summed_all[4], lax.axis_index("chan") * half_width, half_width, 2
    )
    return (agg_map, agg_grad, dw_grad, up_grad, proj_grad, ds_grad)


def solution(mesh):
    in_specs = (
        P(("groups", "rep"), ("slide", "chan"), None),
        P(("groups", "rep"), ("slide", "chan")),
        P(("groups", "rep"), "slide", "chan", None),
        P(),
        P(),
        P(),
        P(),
        P(),
        P(),
        P(),
        P(None, None, "chan"),
    )
    out_specs = (
        P(("groups", "rep"), "slide", "chan", None),
        P("groups", None, "chan"),
        P("groups", None),
        P("groups", None),
        P("groups", None),
        P("groups", None),
    )
    return jax.shard_map(
        on_device, mesh=mesh, in_specs=in_specs, out_specs=out_specs, check_vma=False
    )
```

profile of v0, /device:TPU:0, one launch (start us, length us, event | category | flops | bytes accessed | tf_op | source)
XLA Modules:
  0.0 863.3 jit_solution(13993026256152667323)
XLA Ops:
  18.9 31.2 %pad.226 = bf16[33,257,192]{1,2,0:T(8,128)(2,1)} pad(bf16[16,128,192]{1,2,0:T(8,128)(2,1)} %bitcast.629, bf16[]{:T(256)} %constant.57.clone.1), padding=2_0_1x2_0_1x0_0_0 | pad | bytes 4043138 | tf_op jit(solution)/shard_map/transpose(jvp())/pad | solution.py:68
  50.1 30.9 %pad.227 = bf16[33,257,192]{1,2,0:T(8,128)(2,1)} pad(bf16[16,128,192]{1,2,0:T(8,128)(2,1)} %bitcast.630, bf16[]{:T(256)} %constant.57.clone.1), padding=2_0_1x1_1_1x0_0_0 | pad | bytes 4043138 | tf_op jit(solution)/shard_map/transpose(jvp())/pad | solution.py:68
  81.0 2.2 copy.253
  83.2 31.0 %pad.228 = bf16[33,257,192]{1,2,0:T(8,128)(2,1)} pad(bf16[16,128,192]{1,2,0:T(8,128)(2,1)} %bitcast.631, bf16[]{:T(256)} %constant.57.clone.1), padding=2_0_1x0_2_1x0_0_0 | pad | bytes 4043138 | tf_op jit(solution)/shard_map/transpose(jvp())/pad | solution.py:68
  114.2 2.2 copy.252
  116.4 30.9 %pad.229 = bf16[33,257,192]{1,2,0:T(8,128)(2,1)} pad(bf16[16,128,192]{1,2,0:T(8,128)(2,1)} %bitcast.632, bf16[]{:T(256)} %constant.57.clone.1), padding=1_1_1x2_0_1x0_0_0 | pad | bytes 4043138 | tf_op jit(solution)/shard_map/transpose(jvp())/pad | solution.py:68
  147.3 2.2 copy.251
  149.5 30.9 %pad.230 = bf16[33,257,192]{1,2,0:T(8,128)(2,1)} pad(bf16[16,128,192]{1,2,0:T(8,128)(2,1)} %bitcast.633, bf16[]{:T(256)} %constant.57.clone.1), padding=1_1_1x1_1_1x0_0_0 | pad | bytes 4043138 | tf_op jit(solution)/shard_map/transpose(jvp())/pad | solution.py:68
  181.6 30.9 %pad.231 = bf16[33,257,192]{1,2,0:T(8,128)(2,1)} pad(bf16[16,128,192]{1,2,0:T(8,128)(2,1)} %bitcast.634, bf16[]{:T(256)} %constant.57.clone.1), padding=1_1_1x0_2_1x0_0_0 | pad | bytes 4043138 | tf_op jit(solution)/shard_map/transpose(jvp())/pad | solution.py:68
  212.6 30.6 %pad.232 = bf16[33,257,192]{1,2,0:T(8,128)(2,1)} pad(bf16[16,128,192]{1,2,0:T(8,128)(2,1)S(1)} %bitcast.635, bf16[]{:T(256)} %constant.57.clone.1), padding=0_2_1x2_0_1x0_0_0 | pad | bytes 4043138 | tf_op jit(solution)/shard_map/transpose(jvp())/pad | solution.py:68
  243.4 30.0 %pad.233 = bf16[33,257,192]{1,2,0:T(8,128)(2,1)} pad(bf16[16,128,192]{1,2,0:T(8,128)(2,1)S(1)} %bitcast.636, bf16[]{:T(256)} %constant.57.clone.1), padding=0_2_1x1_1_1x0_0_0 | pad | bytes 4043138 | tf_op jit(solution)/shard_map/transpose(jvp())/pad | solution.py:68
  273.6 30.0 %pad.234 = bf16[33,257,192]{1,2,0:T(8,128)(2,1)} pad(bf16[16,128,192]{1,2,0:T(8,128)(2,1)S(1)} %bitcast.637, bf16[]{:T(256)} %constant.57.clone.1), padding=0_2_1x0_2_1x0_0_0 | pad | bytes 4043138 | tf_op jit(solution)/shard_map/transpose(jvp())/pad | solution.py:68
  303.6 14.5 %add_add_fusion = bf16[33,257,192]{1,2,0:T(8,128)(2,1)S(1)} fusion(bf16[33,257,192]{1,2,0:T(8,128)(2,1)} %pad.234, bf16[33,257,192]{1,2,0:T(8,128)(2,1)} %pad.233, bf16[33,257,192]{1,2,0:T(8,128)(2,1)} %pad.232, bf16[33,257,192]{1,2,0:T(8,128)(2,1)} %pad.231, bf16[33,257,192]{1,2,0:T(8,128)(2,1)} %pad.230, bf16[33,257,192]{1,2,0:T(8,128)(2,1)} %pad.229, ...), kind=kLoop, calls=%fused_computation.105 | loop fusion | flops 13026816 | bytes 32567040 | tf_op jit(solution)/shard_map/transpose(jvp())/add_any | solution.py:68
  318.1 2.3 copy-done.2
  323.3 8.2 all-to-all-start
  331.5 6.3 slice_convert_fusion
  346.7 5.1 all-to-all-start.1
  355.3 2.2 all-to-all-done.1
  359.6 2.3 scatter_custom_fusion.2
  361.9 6.1 reshape.714
  368.0 6.5 copy.108
  374.5 7.6 reshape.715
  382.1 5.5 copy.109
  388.2 3.4 collective-permute-start
  393.3 4.9 convert_element_type.212
  398.2 6.1 copy.132
  404.3 7.1 reshape.736
  411.3 5.8 copy.133
  417.1 8.5 reshape.737
  425.6 3.0 gather_fusion
  431.0 3.3 all-to-all-start.2
  434.4 6.2 fusion.2
  440.5 28.5 %slice.767 = bf16[16,128,192]{1,2,0:T(8,128)(2,1)S(1)} slice(bf16[33,257,192]{1,2,0:T(8,128)(2,1)} %fusion.2), slice={[0:31:2], [0:255:2], [0:192:1]} | slice | bytes 1572864 | tf_op jit(solution)/shard_map/jvp()/slice | solution.py:68
  469.1 28.7 %slice.769 = bf16[16,128,192]{1,2,0:T(8,128)(2,1)} slice(bf16[33,257,192]{1,2,0:T(8,128)(2,1)} %fusion.2), slice={[0:31:2], [1:256:2], [0:192:1]} | slice | bytes 1572864 | tf_op jit(solution)/shard_map/jvp()/slice | solution.py:68
  497.8 28.7 %slice.771 = bf16[16,128,192]{1,2,0:T(8,128)(2,1)} slice(bf16[33,257,192]{1,2,0:T(8,128)(2,1)} %fusion.2), slice={[0:31:2], [2:257:2], [0:192:1]} | slice | bytes 1572864 | tf_op jit(solution)/shard_map/jvp()/slice | solution.py:68
  526.5 28.8 %slice.773 = bf16[16,128,192]{1,2,0:T(8,128)(2,1)} slice(bf16[33,257,192]{1,2,0:T(8,128)(2,1)} %fusion.2), slice={[1:32:2], [0:255:2], [0:192:1]} | slice | bytes 1572864 | tf_op jit(solution)/shard_map/jvp()/slice | solution.py:68
  555.3 28.7 %slice.775 = bf16[16,128,192]{1,2,0:T(8,128)(2,1)} slice(bf16[33,257,192]{1,2,0:T(8,128)(2,1)} %fusion.2), slice={[1:32:2], [1:256:2], [0:192:1]} | slice | bytes 1572864 | tf_op jit(solution)/shard_map/jvp()/slice | solution.py:68
  584.0 28.7 %slice.777 = bf16[16,128,192]{1,2,0:T(8,128)(2,1)} slice(bf16[33,257,192]{1,2,0:T(8,128)(2,1)} %fusion.2), slice={[1:32:2], [2:257:2], [0:192:1]} | slice | bytes 1572864 | tf_op jit(solution)/shard_map/jvp()/slice | solution.py:68
  612.7 28.9 %slice.779 = bf16[16,128,192]{1,2,0:T(8,128)(2,1)} slice(bf16[33,257,192]{1,2,0:T(8,128)(2,1)} %fusion.2), slice={[2:33:2], [0:255:2], [0:192:1]} | slice | bytes 1572864 | tf_op jit(solution)/shard_map/jvp()/slice | solution.py:68
  641.7 28.2 %slice.781 = bf16[16,128,192]{1,2,0:T(8,128)(2,1)S(1)} slice(bf16[33,257,192]{1,2,0:T(8,128)(2,1)} %fusion.2), slice={[2:33:2], [1:256:2], [0:192:1]} | slice | bytes 1572864 | tf_op jit(solution)/shard_map/jvp()/slice | solution.py:68
  669.9 28.3 %slice.783 = bf16[16,128,192]{1,2,0:T(8,128)(2,1)S(1)} slice(bf16[33,257,192]{1,2,0:T(8,128)(2,1)} %fusion.2), slice={[2:33:2], [2:257:2], [0:192:1]} | slice | bytes 1572864 | tf_op jit(solution)/shard_map/jvp()/slice | solution.py:68
  699.9 2.1 fusion.34
  712.9 3.1 dynamic_update_slice.3
  716.1 15.7 %all-reduce.76.cloned.1.call-done = bf16[4,2,2,3072]{3,0,2,1:T(4,128)(2,1)} async-done(((bf16[4,2,2,3072]{3,0,2,1:T(4,128)(2,1)}), bf16[4,2,2,3072]{3,0,2,1:T(4,128)(2,1)}) %all-reduce.76.cloned.1.call-update) | async-done | bytes 98320
  736.6 3.8 multiply_convert_fusion
  750.0 62.6 %psum.36 = f32[49,96]{1,0:T(8,128)} all-reduce(f32[49,96]{1,0:T(8,128)S(1)} %pad_add_fusion), channel_id=1, replica_groups=mesh['groups'=2,'slide'=4,'rep'=2,'chan'=2] {'slide','rep','chan'}, use_global_device_ids=true, to_apply=%region_67.68 | all-reduce | flops 4704 | bytes 37632 | tf_op jit(solution)/shard_map/psum | solution.py:180
  812.6 36.1 %all-reduce.78.cloned.1.call-done = (f32[9,192,192]{2,1,0:T(8,128)}, f32[96,384]{1,0:T(8,128)}, f32[384,96]{0,1:T(8,128)}, f32[384,192]{0,1:T(8,128)}) async-done(((f32[9,192,192]{2,1,0:T(8,128)}, f32[96,384]{1,0:T(8,128)}, f32[384,96]{0,1:T(8,128)}, f32[384,192]{0,1:T(8,128)}), (f32[9,192,192]{2,1,0:T(8,128)}, f32[96,384]{1,0:T(8,128)}, f32[384,96]{0,1:T(8,128)}, ...) | async-done | bytes 1916944 | tf_op jit(solution)/shard_map/psum | solution.py:180
  848.7 2.7 constant_dynamic-slice_fusion
  (210 shorter events, 65.9 us)
Async XLA Ops:
  7.2 336.5 %copy-start = (bf16[384,192]{0,1:T(8,128)(2,1)S(1)}, bf16[384,192]{0,1:T(8,128)(2,1)}, u32[]{:S(2)}) copy-start(bf16[384,192]{0,1:T(8,128)(2,1)} %param.22) | copy-start | bytes 442372
  7.2 5.6 copy-start.10
  303.6 18.2 %copy-start.31 = (s32[1,8]{1,0:T(1,128)S(1)}, s32[1,8]{1,0:T(1,128)}, u32[]{:S(2)}) copy-start(s32[1,8]{1,0:T(1,128)} %param.14) | copy-start | bytes 100
  318.1 2.3 copy-start.2
  320.4 18.1 %copy-start.20 = (f32[49,96]{1,0:T(8,128)S(1)}, f32[49,96]{1,0:T(8,128)}, u32[]{:S(2)}) copy-start(f32[49,96]{1,0:T(8,128)} %param.16) | copy-start | bytes 56452
  320.4 18.1 %copy-start.12 = (bf16[1,8,6144]{2,1,0:T(8,128)(2,1)S(1)}, bf16[1,8,6144]{2,1,0:T(8,128)(2,1)}, u32[]{:S(2)}) copy-start(bf16[1,8,6144]{2,1,0:T(8,128)(2,1)} %param.13) | copy-start | bytes 294916
  320.5 71.1 %collective-permute-start.1 = (bf16[256,192]{0,1:T(8,128)(2,1)S(1)}, bf16[256,192]{0,1:T(8,128)(2,1)}, u32[]{:S(2)}, u32[]{:S(2)}) collective-permute-start(bf16[256,192]{0,1:T(8,128)(2,1)S(1)} %slice_bitcast_fusion), channel_id=1, source_target_pairs={{4,0},{8,4},{12,8},{5,1},{9,5},{13,9},{6,2},{10,6},{14,10},{7,3},{... | collective-permute-start | bytes 294920 | tf_op jit(solution)/shard_map/ppermute | solution.py:18
  323.3 23.4 %all-to-all-start = ((s32[4,2,1]{1,2,0:T(1,128)}), s32[4,2,1]{1,2,0:T(1,128)S(1)}, u32[]{:S(2)}, u32[]{:S(2)}) async-start(s32[4,2,1]{1,2,0:T(1,128)} %bitcast.5), calls=%async_computation | async-start | bytes 4096 | tf_op jit(solution)/shard_map/all_to_all | solution.py:120
  331.5 9.3 %copy-start.26 = (f32[96]{0:T(128)S(1)}, f32[96]{0:T(128)}, u32[]{:S(2)}) copy-start(f32[96]{0:T(128)} %param.17) | copy-start | bytes 1156
  331.5 9.5 %copy-start.22 = (bf16[384,96]{0,1:T(8,128)(2,1)S(1)}, bf16[384,96]{0,1:T(8,128)(2,1)}, u32[]{:S(2)}) copy-start(bf16[384,96]{0,1:T(8,128)(2,1)} %param.19) | copy-start | bytes 221188
  331.5 9.5 %copy-start.24 = (bf16[96,384]{1,0:T(8,128)(2,1)S(1)}, bf16[96,384]{1,0:T(8,128)(2,1)}, u32[]{:S(2)}) copy-start(bf16[96,384]{1,0:T(8,128)(2,1)} %param.18) | copy-start | bytes 221188
  331.5 9.5 %copy-start.28 = (f32[96]{0:T(128)S(1)}, f32[96]{0:T(128)}, u32[]{:S(2)}) copy-start(f32[96]{0:T(128)} %param.20) | copy-start | bytes 1156
  341.0 2.2 copy-start.27
  341.1 4.4 copy-start.29
  346.7 10.8 %all-to-all-start.1 = ((bf16[4,2,3072]{2,1,0:T(2,128)(2,1)}), bf16[4,2,3072]{2,1,0:T(2,128)(2,1)S(1)}, u32[]{:S(2)}, u32[]{:S(2)}) async-start(bf16[4,2,3072]{2,1,0:T(2,128)(2,1)} %all_to_all.25), calls=%async_computation.1 | async-start | bytes 98304 | tf_op jit(solution)/shard_map/all_to_all | solution.py:119
  388.2 46.2 %collective-permute-start = (bf16[256,192]{0,1:T(8,128)(2,1)}, bf16[256,192]{0,1:T(8,128)(2,1)}, u32[]{:S(2)}, u32[]{:S(2)}) collective-permute-start(bf16[256,192]{0,1:T(8,128)(2,1)} %slice_bitcast_fusion.1), channel_id=1, source_target_pairs={{0,4},{4,8},{8,12},{1,5},{5,9},{9,13},{2,6},{6,10},{10,14},{3,7},{... | collective-permute-start | bytes 294920 | tf_op jit(solution)/shard_map/ppermute | solution.py:18
  431.0 280.7 %all-to-all-start.2 = ((bf16[4,4,3072]{2,1,0:T(4,128)(2,1)}), bf16[4,4,3072]{2,1,0:T(4,128)(2,1)S(1)}, u32[]{:S(2)}, u32[]{:S(2)}) async-start(bf16[4,4,3072]{2,1,0:T(4,128)(2,1)} %copy.135), calls=%async_computation.2 | async-start | bytes 196608 | tf_op jit(solution)/shard_map/all_to_all | solution.py:159
  434.3 297.5 %all-reduce.76.cloned.1.call-start = ((), (), s32[]{:S(2)}) async-start(), calls=%async_computation.3 | async-start | bytes 196608
  526.5 171.7 %copy-start.1 = (f32[1,16,96,128]{3,2,1,0:T(8,128)S(1)}, f32[1,16,96,128]{3,2,1,0:T(8,128)}, u32[]{:S(2)}) copy-start(f32[1,16,96,128]{3,2,1,0:T(8,128)} %param.15) | copy-start | bytes 2359300
  698.2 3.8 copy-start.7
  698.2 4.8 copy-start.6
  698.2 5.8 copy-start.5
  698.2 6.8 copy-start.4
  698.6 7.4 copy-start.3
  702.0 5.9 copy-start.8
  702.0 5.9 copy-start.11
  709.5 3.0 copy-start.13
  709.5 3.0 copy-start.14
  709.5 3.0 copy-start.15
  709.5 3.0 copy-start.16
  709.5 3.0 copy-start.17
  709.5 3.0 copy-start.18
  709.6 3.0 copy-start.19
  710.2 23.7 %copy-start.30 = (pred[8]{0:T(512)(128)(4,1)S(1)}, pred[8]{0:T(512)(128)(4,1)}, u32[]{:S(2)}) copy-start(pred[8]{0:T(512)(128)(4,1)} %bitcast_compare_fusion) | copy-start | bytes 28
  710.2 23.8 %copy-start.21 = (f32[49,96]{1,0:T(8,128)S(1)}, f32[49,96]{1,0:T(8,128)}, u32[]{:S(2)}) copy-start(f32[49,96]{1,0:T(8,128)} %param.16) | copy-start | bytes 56452
  712.5 136.2 %all-reduce.78.cloned.1.call-start = ((), (), s32[]{:S(2)}) async-start(), calls=%async_computation.4 | async-start | bytes 4718592 | tf_op jit(solution)/shard_map/psum | solution.py:180
  716.1 24.3 %copy-start.9 = (f32[9,192,192]{2,1,0:T(8,128)}, f32[9,192,192]{2,1,0:T(8,128)S(1)}, u32[]{:S(2)}) copy-start(f32[9,192,192]{2,1,0:T(8,128)S(1)} %dynamic_update_slice.3) | copy-start | bytes 3981316
  736.6 3.8 copy-start.23
  740.4 4.3 copy-start.25
Sparse Core Ops, SparseCore 0:
  712.6 19.1 all-reduce.75
  748.1 100.5 all-reduce.77
where the time goes:
time: 869 us; the launch traced here: 863 us
  local copies, waits for them, and re-layouts  629 us (72%)
  blocking collectives  66.4 us (8%)
  waiting for transfers between devices  54.1 us (6%)
  other arithmetic  44.9 us (5%)
  matrix products  32.1 us (4%)
  starting transfers between devices  21.3 us (2%)
  between operations  16 us (2%)
    pad x9, local copies, waits for them, and re-layouts, aggregate(): padded[row_tap:row_tap + 2 * out_rows - 1:2, col_tap:col_tap + 2 * out_co...  276 us
    slice x9, local copies, waits for them, and re-layouts, aggregate(): padded[row_tap:row_tap + 2 * out_rows - 1:2, col_tap:col_tap + 2 * out_co...  258 us
    psum x1, blocking collectives, on_device(): lax.psum((dw_term, up_term, proj_term, ds_term, embedded), ('slide', 'rep...  62.6 us
    psum x1, waiting for transfers between devices, on_device(): lax.psum((dw_term, up_term, proj_term, ds_term, embedded), ('slide', 'rep...  36.1 us
    dot_general x27, matrix products, aggregate(): jnp.dot(window.reshape(out_rows * out_cols, padded.shape[2]), weight_half...  20.7 us
  transfers between devices with their start and end apart: 7, of which 3 were waited for; matrix products, arithmetic and copies ran while one was open for 42% of the time, Pallas kernels for 0%

commit v1 on v0

--- a/solution.py
+++ b/solution.py
@@ -177,9 +177,10 @@
         agg_term,
         (0, 0, lax.axis_index("chan") * half_width),
     )
-    summed_all = lax.psum(
-        (dw_term, up_term, proj_term, ds_term, embedded), ("slide", "rep", "chan")
-    )
+    number_area = lambda base_x: lax.psum(
+        lax.psum(base_x, axis_name=("rep", "chan")), axis_name="slide"
+    )
+    summed_all = number_area((dw_term, up_term, proj_term, ds_term, embedded))
     dw_grad = summed_all[0]
     up_grad = summed_all[1]
     proj_grad = summed_all[2]

time: 869 us -> 933 us (1.074)
  waiting for transfers between devices: 54.1 us -> 131 us
  blocking collectives: 66.4 us -> 36.1 us
  matrix products: 32.1 us -> 42.2 us
    psum x1 -> x2, waiting for transfers between devices: 36.1 us -> 116 us  [the longest x1 64.9 us: on_device(): lax.psum(lax.psum(base_x, axis_name=('rep', 'chan')), axis_name='slide')]
    psum x1 -> x2, blocking collectives: 62.6 us -> 32.3 us  [the longest x1 21.6 us: on_device(): lax.psum(lax.psum(base_x, axis_name=('rep', 'chan')), axis_name='slide')]
  transfers between devices with their start and end apart: 7 -> 8, of which waited for: 3 -> 4; matrix products, arithmetic and copies ran while one was open for 42% -> 41% of each run, Pallas kernels for 0% -> 0%
where the time goes in v1:
time: 933 us; the launch traced here: 927 us
  local copies, waits for them, and re-layouts  634 us (68%)
  waiting for transfers between devices  131 us (14%)
  other arithmetic  46.2 us (5%)
  matrix products  42.2 us (5%)
  blocking collectives  36.1 us (4%)
  starting transfers between devices  21.3 us (2%)
  between operations  15.8 us (2%)
    pad x9, local copies, waits for them, and re-layouts, aggregate(): padded[row_tap:row_tap + 2 * out_rows - 1:2, col_tap:col_tap + 2 * out_co...  276 us
    slice x9, local copies, waits for them, and re-layouts, aggregate(): padded[row_tap:row_tap + 2 * out_rows - 1:2, col_tap:col_tap + 2 * out_co...  258 us
    psum x1, waiting for transfers between devices, on_device(): lax.psum(lax.psum(base_x, axis_name=('rep', 'chan')), axis_name='slide')  64.9 us
    psum x1, waiting for transfers between devices, on_device(): lax.psum(base_x, axis_name=('rep', 'chan'))  51.5 us
    dot_general x27, matrix products, aggregate(): jnp.dot(window.reshape(out_rows * out_cols, padded.shape[2]), weight_half...  28.8 us
    psum x1, blocking collectives, on_device(): lax.psum(lax.psum(base_x, axis_name=('rep', 'chan')), axis_name='slide')  21.6 us
  transfers between devices with their start and end apart: 8, of which 4 were waited for; matrix products, arithmetic and copies ran while one was open for 41% of the time, Pallas kernels for 0%

profile of v1, /device:TPU:0, one launch (start us, length us, event | category | flops | bytes accessed | tf_op | source)
XLA Modules:
  0.0 927.1 jit_solution(11889875329132915643)
XLA Ops:
  18.9 31.2 %pad.226 = bf16[33,257,192]{1,2,0:T(8,128)(2,1)} pad(bf16[16,128,192]{1,2,0:T(8,128)(2,1)} %bitcast.629, bf16[]{:T(256)} %constant.57.clone.1), padding=2_0_1x2_0_1x0_0_0 | pad | bytes 4043138 | tf_op jit(solution)/shard_map/transpose(jvp())/pad | solution.py:68
  50.1 30.9 %pad.227 = bf16[33,257,192]{1,2,0:T(8,128)(2,1)} pad(bf16[16,128,192]{1,2,0:T(8,128)(2,1)} %bitcast.630, bf16[]{:T(256)} %constant.57.clone.1), padding=2_0_1x1_1_1x0_0_0 | pad | bytes 4043138 | tf_op jit(solution)/shard_map/transpose(jvp())/pad | solution.py:68
  81.0 2.2 copy.253
  83.2 31.0 %pad.228 = bf16[33,257,192]{1,2,0:T(8,128)(2,1)} pad(bf16[16,128,192]{1,2,0:T(8,128)(2,1)} %bitcast.631, bf16[]{:T(256)} %constant.57.clone.1), padding=2_0_1x0_2_1x0_0_0 | pad | bytes 4043138 | tf_op jit(solution)/shard_map/transpose(jvp())/pad | solution.py:68
  114.2 2.2 copy.252
  116.4 30.9 %pad.229 = bf16[33,257,192]{1,2,0:T(8,128)(2,1)} pad(bf16[16,128,192]{1,2,0:T(8,128)(2,1)} %bitcast.632, bf16[]{:T(256)} %constant.57.clone.1), padding=1_1_1x2_0_1x0_0_0 | pad | bytes 4043138 | tf_op jit(solution)/shard_map/transpose(jvp())/pad | solution.py:68
  147.3 2.2 copy.251
  149.5 30.9 %pad.230 = bf16[33,257,192]{1,2,0:T(8,128)(2,1)} pad(bf16[16,128,192]{1,2,0:T(8,128)(2,1)} %bitcast.633, bf16[]{:T(256)} %constant.57.clone.1), padding=1_1_1x1_1_1x0_0_0 | pad | bytes 4043138 | tf_op jit(solution)/shard_map/transpose(jvp())/pad | solution.py:68
  181.6 30.9 %pad.231 = bf16[33,257,192]{1,2,0:T(8,128)(2,1)} pad(bf16[16,128,192]{1,2,0:T(8,128)(2,1)} %bitcast.634, bf16[]{:T(256)} %constant.57.clone.1), padding=1_1_1x0_2_1x0_0_0 | pad | bytes 4043138 | tf_op jit(solution)/shard_map/transpose(jvp())/pad | solution.py:68
  212.6 30.6 %pad.232 = bf16[33,257,192]{1,2,0:T(8,128)(2,1)} pad(bf16[16,128,192]{1,2,0:T(8,128)(2,1)S(1)} %bitcast.635, bf16[]{:T(256)} %constant.57.clone.1), padding=0_2_1x2_0_1x0_0_0 | pad | bytes 4043138 | tf_op jit(solution)/shard_map/transpose(jvp())/pad | solution.py:68
  243.4 30.0 %pad.233 = bf16[33,257,192]{1,2,0:T(8,128)(2,1)} pad(bf16[16,128,192]{1,2,0:T(8,128)(2,1)S(1)} %bitcast.636, bf16[]{:T(256)} %constant.57.clone.1), padding=0_2_1x1_1_1x0_0_0 | pad | bytes 4043138 | tf_op jit(solution)/shard_map/transpose(jvp())/pad | solution.py:68
  273.6 30.0 %pad.234 = bf16[33,257,192]{1,2,0:T(8,128)(2,1)} pad(bf16[16,128,192]{1,2,0:T(8,128)(2,1)S(1)} %bitcast.637, bf16[]{:T(256)} %constant.57.clone.1), padding=0_2_1x0_2_1x0_0_0 | pad | bytes 4043138 | tf_op jit(solution)/shard_map/transpose(jvp())/pad | solution.py:68
  303.6 14.5 %add_add_fusion = bf16[33,257,192]{1,2,0:T(8,128)(2,1)S(1)} fusion(bf16[33,257,192]{1,2,0:T(8,128)(2,1)} %pad.234, bf16[33,257,192]{1,2,0:T(8,128)(2,1)} %pad.233, bf16[33,257,192]{1,2,0:T(8,128)(2,1)} %pad.232, bf16[33,257,192]{1,2,0:T(8,128)(2,1)} %pad.231, bf16[33,257,192]{1,2,0:T(8,128)(2,1)} %pad.230, bf16[33,257,192]{1,2,0:T(8,128)(2,1)} %pad.229, ...), kind=kLoop, calls=%fused_computation.105 | loop fusion | flops 13026816 | bytes 32567040 | tf_op jit(solution)/shard_map/transpose(jvp())/add_any | solution.py:68
  318.1 2.3 copy-done.2
  323.3 8.2 all-to-all-start
  331.5 6.3 slice_convert_fusion
  346.2 5.1 all-to-all-start.1
  359.0 2.3 scatter_custom_fusion.2
  361.4 6.1 reshape.714
  367.5 6.5 copy.108
  374.0 7.6 reshape.715
  381.5 5.5 copy.109
  387.6 3.4 collective-permute-start
  392.7 4.9 convert_element_type.212
  397.6 6.1 copy.132
  403.7 7.1 reshape.736
  410.8 5.8 copy.133
  416.6 8.5 reshape.737
  425.1 3.0 gather_fusion
  430.4 3.3 all-to-all-start.2
  433.8 6.2 fusion.2
  440.0 28.5 %slice.767 = bf16[16,128,192]{1,2,0:T(8,128)(2,1)S(1)} slice(bf16[33,257,192]{1,2,0:T(8,128)(2,1)} %fusion.2), slice={[0:31:2], [0:255:2], [0:192:1]} | slice | bytes 1572864 | tf_op jit(solution)/shard_map/jvp()/slice | solution.py:68
  468.5 28.7 %slice.769 = bf16[16,128,192]{1,2,0:T(8,128)(2,1)} slice(bf16[33,257,192]{1,2,0:T(8,128)(2,1)} %fusion.2), slice={[0:31:2], [1:256:2], [0:192:1]} | slice | bytes 1572864 | tf_op jit(solution)/shard_map/jvp()/slice | solution.py:68
  497.2 28.7 %slice.771 = bf16[16,128,192]{1,2,0:T(8,128)(2,1)} slice(bf16[33,257,192]{1,2,0:T(8,128)(2,1)} %fusion.2), slice={[0:31:2], [2:257:2], [0:192:1]} | slice | bytes 1572864 | tf_op jit(solution)/shard_map/jvp()/slice | solution.py:68
  525.9 28.8 %slice.773 = bf16[16,128,192]{1,2,0:T(8,128)(2,1)} slice(bf16[33,257,192]{1,2,0:T(8,128)(2,1)} %fusion.2), slice={[1:32:2], [0:255:2], [0:192:1]} | slice | bytes 1572864 | tf_op jit(solution)/shard_map/jvp()/slice | solution.py:68
  554.7 28.7 %slice.775 = bf16[16,128,192]{1,2,0:T(8,128)(2,1)} slice(bf16[33,257,192]{1,2,0:T(8,128)(2,1)} %fusion.2), slice={[1:32:2], [1:256:2], [0:192:1]} | slice | bytes 1572864 | tf_op jit(solution)/shard_map/jvp()/slice | solution.py:68
  583.4 28.8 %slice.777 = bf16[16,128,192]{1,2,0:T(8,128)(2,1)} slice(bf16[33,257,192]{1,2,0:T(8,128)(2,1)} %fusion.2), slice={[1:32:2], [2:257:2], [0:192:1]} | slice | bytes 1572864 | tf_op jit(solution)/shard_map/jvp()/slice | solution.py:68
  612.2 28.9 %slice.779 = bf16[16,128,192]{1,2,0:T(8,128)(2,1)} slice(bf16[33,257,192]{1,2,0:T(8,128)(2,1)} %fusion.2), slice={[2:33:2], [0:255:2], [0:192:1]} | slice | bytes 1572864 | tf_op jit(solution)/shard_map/jvp()/slice | solution.py:68
  641.1 28.2 %slice.781 = bf16[16,128,192]{1,2,0:T(8,128)(2,1)S(1)} slice(bf16[33,257,192]{1,2,0:T(8,128)(2,1)} %fusion.2), slice={[2:33:2], [1:256:2], [0:192:1]} | slice | bytes 1572864 | tf_op jit(solution)/shard_map/jvp()/slice | solution.py:68
  669.3 28.3 %slice.783 = bf16[16,128,192]{1,2,0:T(8,128)(2,1)S(1)} slice(bf16[33,257,192]{1,2,0:T(8,128)(2,1)} %fusion.2), slice={[2:33:2], [2:257:2], [0:192:1]} | slice | bytes 1572864 | tf_op jit(solution)/shard_map/jvp()/slice | solution.py:68
  715.7 5.0 dynamic_update_slice.3
  720.6 12.7 %all-reduce.78.cloned.1.call-done = bf16[4,2,2,3072]{3,0,2,1:T(4,128)(2,1)} async-done(((bf16[4,2,2,3072]{3,0,2,1:T(4,128)(2,1)}), bf16[4,2,2,3072]{3,0,2,1:T(4,128)(2,1)}) %all-reduce.78.cloned.1.call-update) | async-done | bytes 98320
  738.2 3.8 multiply_convert_fusion
  761.0 51.5 %all-reduce.80.cloned.1.call-done = (f32[9,192,192]{2,1,0:T(8,128)}, f32[96,384]{1,0:T(8,128)}, f32[384,96]{0,1:T(8,128)}, f32[384,192]{0,1:T(8,128)}) async-done(((f32[9,192,192]{2,1,0:T(8,128)}, f32[96,384]{1,0:T(8,128)}, f32[384,96]{0,1:T(8,128)}, f32[384,192]{0,1:T(8,128)}), (f32[9,192,192]{2,1,0:T(8,128)}, f32[96,384]{1,0:T(8,128)}, f32[384,96]{0,1:T(8,128)}, ...) | async-done | bytes 1916944 | tf_op jit(solution)/shard_map/psum | solution.py:181
  815.6 10.7 %psum.72 = f32[49,96]{1,0:T(8,128)S(1)} all-reduce(f32[49,96]{1,0:T(8,128)S(1)} %pad_add_fusion), channel_id=1, replica_groups=mesh['groups'=2,'slide'=4,'rep'=2,'chan'=2] {'rep','chan'}, use_global_device_ids=true, to_apply=%region_68.69 | all-reduce | flops 4704 | bytes 37632 | tf_op jit(solution)/shard_map/psum | solution.py:181
  826.3 21.6 %psum.73 = f32[49,96]{1,0:T(8,128)} all-reduce(f32[49,96]{1,0:T(8,128)S(1)} %psum.72), channel_id=1, replica_groups=mesh['groups'=2,'slide'=4,'rep'=2,'chan'=2] {'slide'}, use_global_device_ids=true, to_apply=%region_69.70 | all-reduce | flops 4704 | bytes 37632 | tf_op jit(solution)/shard_map/psum | solution.py:180
  847.9 64.9 %all-reduce.82.cloned.1.call-done = (f32[9,192,192]{2,1,0:T(8,128)}, f32[96,384]{1,0:T(8,128)}, f32[384,96]{0,1:T(8,128)}, f32[384,192]{0,1:T(8,128)}) async-done(((f32[9,192,192]{2,1,0:T(8,128)}, f32[96,384]{1,0:T(8,128)}, f32[384,96]{0,1:T(8,128)}, f32[384,192]{0,1:T(8,128)}), (f32[9,192,192]{2,1,0:T(8,128)}, f32[96,384]{1,0:T(8,128)}, f32[384,96]{0,1:T(8,128)}, ...) | async-done | bytes 1916944 | tf_op jit(solution)/shard_map/psum | solution.py:180
  912.8 2.7 constant_dynamic-slice_fusion
  (228 shorter events, 85.4 us)
Async XLA Ops:
  7.2 335.9 %copy-start = (bf16[384,192]{0,1:T(8,128)(2,1)S(1)}, bf16[384,192]{0,1:T(8,128)(2,1)}, u32[]{:S(2)}) copy-start(bf16[384,192]{0,1:T(8,128)(2,1)} %param.22) | copy-start | bytes 442372
  7.2 5.6 copy-start.10
  303.6 18.2 %copy-start.38 = (s32[1,8]{1,0:T(1,128)S(1)}, s32[1,8]{1,0:T(1,128)}, u32[]{:S(2)}) copy-start(s32[1,8]{1,0:T(1,128)} %param.14) | copy-start | bytes 100
  318.1 2.3 copy-start.2
  320.4 17.5 %copy-start.27 = (f32[49,96]{1,0:T(8,128)S(1)}, f32[49,96]{1,0:T(8,128)}, u32[]{:S(2)}) copy-start(f32[49,96]{1,0:T(8,128)} %param.16) | copy-start | bytes 56452
  320.4 17.5 %copy-start.14 = (bf16[1,8,6144]{2,1,0:T(8,128)(2,1)S(1)}, bf16[1,8,6144]{2,1,0:T(8,128)(2,1)}, u32[]{:S(2)}) copy-start(bf16[1,8,6144]{2,1,0:T(8,128)(2,1)} %param.13) | copy-start | bytes 294916
  320.5 70.5 %collective-permute-start.1 = (bf16[256,192]{0,1:T(8,128)(2,1)S(1)}, bf16[256,192]{0,1:T(8,128)(2,1)}, u32[]{:S(2)}, u32[]{:S(2)}) collective-permute-start(bf16[256,192]{0,1:T(8,128)(2,1)S(1)} %slice_bitcast_fusion), channel_id=1, source_target_pairs={{4,0},{8,4},{12,8},{5,1},{9,5},{13,9},{6,2},{10,6},{14,10},{7,3},{... | collective-permute-start | bytes 294920 | tf_op jit(solution)/shard_map/ppermute | solution.py:18
  323.3 22.9 %all-to-all-start = ((s32[4,2,1]{1,2,0:T(1,128)}), s32[4,2,1]{1,2,0:T(1,128)S(1)}, u32[]{:S(2)}, u32[]{:S(2)}) async-start(s32[4,2,1]{1,2,0:T(1,128)} %bitcast.5), calls=%async_computation | async-start | bytes 4096 | tf_op jit(solution)/shard_map/all_to_all | solution.py:120
  331.5 8.8 copy-start.33
  331.5 9.0 copy-start.29
  331.5 9.0 copy-start.31
  331.5 9.0 copy-start.36
  340.5 2.2 copy-start.35
  340.5 4.4 copy-start.37
  346.2 10.8 %all-to-all-start.1 = ((bf16[4,2,3072]{2,1,0:T(2,128)(2,1)}), bf16[4,2,3072]{2,1,0:T(2,128)(2,1)S(1)}, u32[]{:S(2)}, u32[]{:S(2)}) async-start(bf16[4,2,3072]{2,1,0:T(2,128)(2,1)} %all_to_all.25), calls=%async_computation.1 | async-start | bytes 98304 | tf_op jit(solution)/shard_map/all_to_all | solution.py:119
  387.6 46.2 %collective-permute-start = (bf16[256,192]{0,1:T(8,128)(2,1)}, bf16[256,192]{0,1:T(8,128)(2,1)}, u32[]{:S(2)}, u32[]{:S(2)}) collective-permute-start(bf16[256,192]{0,1:T(8,128)(2,1)} %slice_bitcast_fusion.1), channel_id=1, source_target_pairs={{0,4},{4,8},{8,12},{1,5},{5,9},{9,13},{2,6},{6,10},{10,14},{3,7},{... | collective-permute-start | bytes 294920 | tf_op jit(solution)/shard_map/ppermute | solution.py:18
  430.4 282.8 %all-to-all-start.2 = ((bf16[4,4,3072]{2,1,0:T(4,128)(2,1)}), bf16[4,4,3072]{2,1,0:T(4,128)(2,1)S(1)}, u32[]{:S(2)}, u32[]{:S(2)}) async-start(bf16[4,4,3072]{2,1,0:T(4,128)(2,1)} %copy.135), calls=%async_computation.2 | async-start | bytes 196608 | tf_op jit(solution)/shard_map/all_to_all | solution.py:159
  433.7 299.6 %all-reduce.78.cloned.1.call-start = ((), (), s32[]{:S(2)}) async-start(), calls=%async_computation.3 | async-start | bytes 196608
  525.9 171.7 %copy-start.1 = (f32[1,16,96,128]{3,2,1,0:T(8,128)S(1)}, f32[1,16,96,128]{3,2,1,0:T(8,128)}, u32[]{:S(2)}) copy-start(f32[1,16,96,128]{3,2,1,0:T(8,128)} %param.15) | copy-start | bytes 2359300
  697.6 3.8 copy-start.8
  697.6 4.8 copy-start.7
  697.7 5.8 copy-start.6
  697.7 6.8 copy-start.5
  698.0 7.4 copy-start.3
  701.5 5.9 copy-start.9
  708.5 5.6 copy-start.20
  708.5 5.6 copy-start.21
  708.5 5.6 copy-start.22
  708.5 5.6 copy-start.23
  708.5 5.6 copy-start.24
  708.5 5.6 copy-start.25
  708.5 5.6 copy-start.26
  710.9 24.7 %copy-start.28 = (f32[49,96]{1,0:T(8,128)S(1)}, f32[49,96]{1,0:T(8,128)}, u32[]{:S(2)}) copy-start(f32[49,96]{1,0:T(8,128)} %param.16) | copy-start | bytes 56452
  714.0 98.4 %all-reduce.80.cloned.1.call-start = ((), (), s32[]{:S(2)}) async-start(), calls=%async_computation.4 | async-start | bytes 4718592 | tf_op jit(solution)/shard_map/psum | solution.py:181
  737.8 4.2 copy-start.18
  738.2 3.8 copy-start.16
  738.2 3.8 copy-start.30
  742.0 5.4 copy-start.11
  743.0 1.3 copy-start.15
  747.0 6.9 copy-start.17
  749.2 7.4 copy-start.4
  753.2 0.7 copy-start.12
  754.9 157.9 %all-reduce.82.cloned.1.call-start = ((), (), s32[]{:S(2)}) async-start(), calls=%async_computation.5 | async-start | bytes 4718592 | tf_op jit(solution)/shard_map/psum | solution.py:180
  756.7 55.8 %copy-start.32 = (bf16[96,384]{1,0:T(8,128)(2,1)S(1)}, bf16[96,384]{1,0:T(8,128)(2,1)}, u32[]{:S(2)}) copy-start(bf16[96,384]{1,0:T(8,128)(2,1)} %param.18) | copy-start | bytes 221188
  757.8 54.6 %copy-start.13 = (bf16[512,384]{1,0:T(8,128)(2,1)S(1)}, bf16[512,384]{1,0:T(8,128)(2,1)}, u32[]{:S(2)}) copy-start(bf16[512,384]{1,0:T(8,128)(2,1)} %copy-done.12) | copy-start | bytes 1179652
  757.8 55.0 %copy-start.34 = (f32[96]{0:T(128)S(1)}, f32[96]{0:T(128)}, u32[]{:S(2)}) copy-start(f32[96]{0:T(128)} %param.17) | copy-start | bytes 1156
  757.8 55.3 %copy-start.19 = (f32[8,8,8]{2,1,0:T(8,128)S(1)}, f32[8,8,8]{2,1,0:T(8,128)}, u32[]{:S(2)}) copy-start(f32[8,8,8]{2,1,0:T(8,128)} %copy-done.18) | copy-start | bytes 6148
Sparse Core Ops, SparseCore 0:
  714.1 19.2 all-reduce.77
  755.0 57.3 all-reduce.79
  815.0 97.7 all-reduce.81
